TPU v7x, 256 devices: a whole 4x4x8 slice. The times are simulated.
256 devices in a mesh: grp: 8 (over y, x_lo), ctx: 32 (over z, x_hi, core).
Axes of the slice: x: 4 (x_hi: 2, x_lo: 2; x = x_hi * 2 + x_lo), y: 4, z: 8, core: 2. Of those that a mesh axis runs over, the one named last changes fastest.
Arguments:
- tokens: bfloat16 [8, 2048, 4096], P('grp', 'ctx'), may hold values from -8 to 8
- req_lengths: int32 [8, 8], replicated, may hold values from 1 to 1088, 2048 in all within a row
- req_adapter: int32 [8, 8], replicated, may hold values from 0 to 7
- adapter_slot: int32 [8], replicated, may hold values from 0 to 7, each once
- query_weight: bfloat16 [4096, 4096], P(None, 'grp'), may hold values from -0.109375 to 0.109375
- key_weight: bfloat16 [4096, 1024], P(None, 'grp'), may hold values from -0.109375 to 0.109375
- value_weight: bfloat16 [4096, 1024], P(None, 'grp'), may hold values from -0.09375 to 0.09375
- w_out: bfloat16 [4096, 4096], P('grp'), may hold values from -0.09375 to 0.09375
- down_qkv: bfloat16 [8, 48, 4096], P('grp'), may hold values from -0.09375 to 0.09375
- up_query: bfloat16 [8, 16, 4096], P('grp'), may hold values from -0.59765625 to 0.59765625
- up_kv: bfloat16 [8, 2, 16, 1024], P('grp'), may hold values from -0.59765625 to 0.59765625
- down_out: bfloat16 [8, 16, 4096], P('grp'), may hold values from -0.09375 to 0.09375
- up_out: bfloat16 [8, 16, 4096], P('grp'), may hold values from -0.59765625 to 0.59765625
Outputs:
- mixed: bfloat16 [8, 2048, 4096], P('grp', 'ctx')
Inputs may be any that keep to these rules, and one draw needn't show every extreme that they name: `req_lengths`: row b holds the lengths of group b's 8 requests in order; each row sums to 2048 and its longest request has 1088 positions. adapter a's tables stand at slot adapter_slot[a]; every slot is used by one adapter.
All inputs are finite; a program needn't handle non-finite values.
Results may differ from a plain program's by a relative error of at most 0.015.
The roundings to bfloat16 on the way count: a program that leaves them out, or rounds other values in their place, can miss the bound.
Values may be sent and summed in bfloat16 or wider, within the bound.
A program may use at most 128 MiB of HBM per device.

v0:
```python
import math
import jax
import jax.numpy as jnp
from jax import lax
from jax.sharding import PartitionSpec as P

MODEL_WIDTH = 4096
HD = 128
ADAPTER_RANK = 16
ROPE_BASE = 500000.0
ADAPTER_SCALE = 2.0
MASKED_SCORE = -1e30


def request_info(lengths, adapter_ids, positions):
    req_ends = jnp.cumsum(lengths, axis=-1)
    starts = req_ends - lengths
    segment = jnp.sum((req_ends[..., None, :] <= positions[:, None]).astype(jnp.int32), axis=-1)
    req_picks = (segment[..., None] == jnp.arange(lengths.shape[-1], dtype=jnp.int32)).astype(
        jnp.int32
    )
    req_begin = jnp.sum(req_picks * starts[..., None, :], axis=-1)
    req_owner = jnp.sum(req_picks * adapter_ids[..., None, :], axis=-1)
    return (segment, req_begin, req_owner)


def rotate(values, offsets):
    half_width = values.shape[-1] // 2
    frequency = jnp.exp(
        jnp.arange(half_width, dtype=jnp.float32) * (-2.0 * math.log(ROPE_BASE) / values.shape[-1])
    )
    angles = offsets[..., None, None] * frequency
    cosine = jnp.cos(angles)
    sine = jnp.sin(angles)
    lower_half = values[..., :half_width]
    upper_half = values[..., half_width:]
    return jnp.concatenate(
        [lower_half * cosine - upper_half * sine, upper_half * cosine + lower_half * sine], axis=-1
    )


def widen_rows(adapter_middle, adapter_onehot, upward_table):
    masked_scores = adapter_onehot[:, :, None] * adapter_middle[:, None, :]
    flat_rows = masked_scores.reshape(
        masked_scores.shape[0], upward_table.shape[0] * upward_table.shape[1]
    )
    return jnp.dot(
        flat_rows,
        upward_table.reshape(upward_table.shape[0] * upward_table.shape[1], upward_table.shape[2]),
        preferred_element_type=jnp.float32,
    )


def narrow_rows(input_rows, down_table, adapter_onehot):
    every_term = jnp.einsum(
        "gtd,afd->gtaf", input_rows, down_table, preferred_element_type=jnp.float32
    )
    return jnp.sum(every_term * adapter_onehot[..., None].astype(jnp.float32), axis=2).astype(
        jnp.bfloat16
    )


def body(
    tokens,
    req_lengths,
    req_adapter,
    adapter_slot,
    query_weight,
    key_weight,
    value_weight,
    w_out,
    down_qkv,
    up_query,
    up_kv,
    down_out,
    up_out,
):
    groups = req_lengths.shape[0]
    token_matrix = tokens.shape[1]
    adapters = adapter_slot.shape[0]
    group_index = lax.axis_index("grp")
    block_index = lax.axis_index("ctx")
    q_cols = query_weight.shape[1]
    kv_cols = key_weight.shape[1]
    kv_local = kv_cols // HD
    heads_per_kv = q_cols // kv_cols
    positions = block_index * token_matrix + jnp.arange(token_matrix, dtype=jnp.int32)
    seg_rows, begin_rows, owner_rows = request_info(req_lengths, req_adapter, positions)
    onehot_rows = (owner_rows[..., None] == jnp.arange(adapters, dtype=jnp.int32)).astype(
        jnp.bfloat16
    )
    own_hot = lax.dynamic_slice_in_dim(onehot_rows, group_index, 1, 0)
    down_slots, upq_slots, upkv_slots, downo_slots, upo_slots = (
        lax.all_gather(down_qkv, "grp", axis=0, tiled=True),
        lax.all_gather(up_query, "grp", axis=0, tiled=True),
        lax.all_gather(up_kv, "grp", axis=0, tiled=True),
        lax.all_gather(down_out, "grp", axis=0, tiled=True),
        lax.all_gather(up_out, "grp", axis=0, tiled=True),
    )
    upq_slots = lax.dynamic_slice_in_dim(upq_slots, group_index * q_cols, q_cols, 2)
    upkv_slots = lax.dynamic_slice_in_dim(upkv_slots, group_index * kv_cols, kv_cols, 3)
    downo_slots = lax.dynamic_slice_in_dim(downo_slots, group_index * q_cols, q_cols, 2)
    down_adapter = jnp.take(down_slots, adapter_slot, axis=0)
    up_query_adapter = jnp.take(upq_slots, adapter_slot, axis=0)
    up_key_value_adapter = jnp.take(upkv_slots, adapter_slot, axis=0)
    downo_ad = jnp.take(downo_slots, adapter_slot, axis=0)
    up_output_adapter = jnp.take(upo_slots, adapter_slot, axis=0)
    all_requests = lax.all_gather(tokens, "grp", axis=0, tiled=True)
    adapter_middle = narrow_rows(all_requests, down_adapter, onehot_rows)
    count_of_rows = groups * token_matrix
    flat_inputs = all_requests.reshape(count_of_rows, MODEL_WIDTH)
    onehot_flat = onehot_rows.reshape(count_of_rows, adapters)
    middle_flat = adapter_middle.reshape(count_of_rows, 3 * ADAPTER_RANK)
    offsets = (positions[None, :] - begin_rows).astype(jnp.float32).reshape(count_of_rows)
    query_total = jnp.dot(
        flat_inputs, query_weight, preferred_element_type=jnp.float32
    ) + ADAPTER_SCALE * widen_rows(middle_flat[:, 0:ADAPTER_RANK], onehot_flat, up_query_adapter)
    key_total = jnp.dot(
        flat_inputs, key_weight, preferred_element_type=jnp.float32
    ) + ADAPTER_SCALE * widen_rows(
        middle_flat[:, ADAPTER_RANK : 2 * ADAPTER_RANK], onehot_flat, up_key_value_adapter[:, 0]
    )
    value_total = jnp.dot(
        flat_inputs, value_weight, preferred_element_type=jnp.float32
    ) + ADAPTER_SCALE * widen_rows(
        middle_flat[:, 2 * ADAPTER_RANK : 3 * ADAPTER_RANK], onehot_flat, up_key_value_adapter[:, 1]
    )
    query = rotate(query_total.reshape(count_of_rows, q_cols // HD, HD), offsets).astype(
        jnp.bfloat16
    )
    query = query.reshape(groups, token_matrix, kv_local, heads_per_kv, HD)
    key = (
        rotate(key_total.reshape(count_of_rows, kv_local, HD), offsets)
        .astype(jnp.bfloat16)
        .reshape(groups, token_matrix, kv_cols)
    )
    value = value_total.astype(jnp.bfloat16).reshape(groups, token_matrix, kv_cols)
    score_scale = math.sqrt(HD)
    start_top = jnp.full((groups, token_matrix, kv_local, heads_per_kv), MASKED_SCORE, jnp.float32)
    key_piece = lax.all_gather(key, "ctx", axis=1, tiled=True)
    value_piece = lax.all_gather(value, "ctx", axis=1, tiled=True)
    key_count = key_piece.shape[1]
    key_positions = jnp.arange(key_count, dtype=jnp.int32)
    key_segment, unused_begin, unused_owner = request_info(req_lengths, req_adapter, key_positions)
    allowed = (
        (key_segment[:, None, :] == seg_rows[:, :, None])
        & (key_positions[None, None, :] <= positions[None, :, None])
        & (key_positions[None, None, :] >= 0)
    )
    key_heads = key_piece.reshape(groups, key_count, kv_local, HD)
    value_heads = value_piece.reshape(groups, key_count, kv_local, HD)
    scores = (
        jnp.einsum("gtkjd,gskd->gtkjs", query, key_heads, preferred_element_type=jnp.float32)
        / score_scale
    )
    mask_full = allowed[:, :, None, None, :]
    scores = jnp.where(mask_full, scores, MASKED_SCORE)
    new_top = jnp.maximum(start_top, jnp.max(scores, axis=-1))
    weights = jnp.where(mask_full, jnp.exp(scores - new_top[..., None]), 0.0)
    new_sum = jnp.sum(weights, axis=-1)
    new_accum = jnp.einsum(
        "gtkjs,gskd->gtkjd",
        weights.astype(jnp.bfloat16),
        value_heads,
        preferred_element_type=jnp.float32,
    )
    final_state = (new_top, new_sum, new_accum)
    final_top, final_sum, final_accum = final_state
    attended = (
        (final_accum / final_sum[..., None])
        .astype(jnp.bfloat16)
        .reshape(groups, token_matrix, q_cols)
    )
    attended_flat = attended.reshape(count_of_rows, q_cols)
    mid_terms = jnp.einsum(
        "pc,arc->par", attended_flat, downo_ad, preferred_element_type=jnp.float32
    )
    out_terms = jnp.sum(mid_terms * onehot_flat[..., None].astype(jnp.float32), axis=1).reshape(
        groups, token_matrix, ADAPTER_RANK
    )
    output_middle = lax.psum_scatter(
        out_terms.astype(jnp.bfloat16), "grp", scatter_dimension=0, tiled=True
    )
    partial_term = jnp.einsum("gtc,cd->gtd", attended, w_out, preferred_element_type=jnp.float32)
    base_product = lax.psum_scatter(
        lax.optimization_barrier(partial_term.astype(jnp.bfloat16))
        .astype(jnp.float32)
        .astype(jnp.bfloat16),
        "grp",
        scatter_dimension=0,
        tiled=True,
    ).astype(jnp.float32)
    adapter_delta = widen_rows(
        output_middle.reshape(token_matrix, ADAPTER_RANK),
        own_hot.reshape(token_matrix, adapters),
        up_output_adapter,
    )
    return (
        base_product + ADAPTER_SCALE * adapter_delta.reshape(1, token_matrix, MODEL_WIDTH)
    ).astype(jnp.bfloat16)


def solution(mesh):
    placed = (
        P("grp", "ctx", None),
        P(),
        P(),
        P(),
        P(None, "grp"),
        P(None, "grp"),
        P(None, "grp"),
        P("grp", None),
        P("grp", None, None),
        P("grp", None, None),
        P("grp", None, None, None),
        P("grp", None, None),
        P("grp", None, None),
    )
    return jax.shard_map(
        body, mesh=mesh, in_specs=placed, out_specs=P("grp", "ctx", None), check_vma=False
    )
```

profile of v0, /device:TPU:1, one launch (start us, length us, event | category | flops | bytes accessed | tf_op | source)
XLA Modules:
  0.0 638.5 jit_solution(13202051979169333373)
XLA Ops:
  13.3 29.5 %all_gather.26 = bf16[8,2,16,1024]{3,2,1,0:T(8,128)(2,1)S(1)} all-gather(bf16[1,2,16,1024]{3,2,1,0:T(8,128)(2,1)} %param.25), channel_id=1, replica_groups=mesh['grp'=8,'ctx'=32] {'grp'}, dimensions={0}, use_global_device_ids=true | all-gather | bytes 589824 | tf_op jit(solution)/shard_map/all_gather | solution.py:96
  43.5 49.3 %all-gather.10.cloned.1.call-done = bf16[8,48,4096]{2,1,0:T(8,128)(2,1)} async-done(((bf16[1,48,4096]{2,1,0:T(8,128)(2,1)}), bf16[8,48,4096]{2,1,0:T(8,128)(2,1)}) %all-gather.10.cloned.1.call-update) | async-done | bytes 3145744 | tf_op jit(solution)/shard_map/all_gather | solution.py:94
  92.8 4.3 gather_fusion
  97.1 91.1 %all-gather.8.cloned.1.call-done = bf16[8,64,4096]{2,1,0:T(8,128)(2,1)} async-done(((bf16[1,64,4096]{2,1,0:T(8,128)(2,1)}), bf16[8,64,4096]{2,1,0:T(8,128)(2,1)}) %all-gather.8.cloned.1.call-update) | async-done | bytes 4194320 | tf_op jit(solution)/shard_map/all_gather | solution.py:108
  188.2 6.2 fusion.20
  194.7 3.5 fusion.88
  198.4 1.2 fusion.58
  200.5 3.5 fusion.87
  207.4 20.7 %all-gather.16.cloned.1.call-done = bf16[8,16,4096]{2,1,0:T(8,128)(2,1)} async-done(((bf16[1,16,4096]{2,1,0:T(8,128)(2,1)}), bf16[8,16,4096]{2,1,0:T(8,128)(2,1)}) %all-gather.16.cloned.1.call-update) | async-done | bytes 1048592 | tf_op jit(solution)/shard_map/all_gather | solution.py:95
  228.1 0.9 constant_dynamic-slice_fusion
  229.6 42.5 %all-gather.18.cloned.1.call-done = bf16[8,16,4096]{2,1,0:T(8,128)(2,1)} async-done(((bf16[1,16,4096]{2,1,0:T(8,128)(2,1)}), bf16[8,16,4096]{2,1,0:T(8,128)(2,1)}) %all-gather.18.cloned.1.call-update) | async-done | bytes 1048592 | tf_op jit(solution)/shard_map/all_gather | solution.py:97
  272.1 0.9 constant_dynamic-slice_fusion.2
  273.5 5.8 fusion.89
  281.4 84.8 %all-gather.14.cloned.1.call-done = bf16[8,2048,128]{2,1,0:T(8,128)(2,1)} async-done(((bf16[8,64,128]{2,1,0:T(8,128)(2,1)}), bf16[8,2048,128]{2,1,0:T(8,128)(2,1)}) %all-gather.14.cloned.1.call-update) | async-done | bytes 4194320 | tf_op jit(solution)/shard_map/all_gather | solution.py:140
  366.2 10.0 %fusion = (f32[8,64,4]{1,2,0:T(4,128)S(1)}, f32[8,2048,64,4]{1,2,3,0:T(8,128)}) fusion(pred[8,64,2048]{2,1,0:T(8,128)(4,1)S(1)} %compare_and_fusion, bf16[8,64,4,64]{3,1,2,0:T(8,128)(2,1)S(1)} %copy.52, bf16[8,64,4,64]{3,1,2,0:T(8,128)(2,1)S(1)} %copy.51, bf16[8,2048,128]{2,1,0:T(8,128)(2,1)} %all-gather.14.cloned.1.call-done), kind=kOutput, calls=%fused_computation.7 | convolution fusion | flops 1087371264 | bytes 22552576 | tf_op jit(solution)/shard_map/gtkjd,gskd->gtkjs/dot_general | solution.py:153
  376.2 8.7 %fusion.1 = f32[8,64,4]{1,2,0:T(4,128)S(1)} fusion(f32[8,2048,64,4]{1,2,3,0:T(8,128)} %get-tuple-element.26, f32[8,64,4]{1,2,0:T(4,128)S(1)} %broadcast_maximum_fusion, pred[8,64,2048]{2,1,0:T(8,128)(4,1)S(1)} %compare_and_fusion), kind=kLoop, calls=%fused_computation.8 | loop fusion | flops 20969472 | bytes 17842176 | tf_op jit(solution)/shard_map/reduce_sum | solution.py:160
  384.8 67.4 %all-gather.12.cloned.1.call-done = bf16[8,2048,128]{2,1,0:T(8,128)(2,1)} async-done(((bf16[8,64,128]{2,1,0:T(8,128)(2,1)}), bf16[8,2048,128]{2,1,0:T(8,128)(2,1)}) %all-gather.12.cloned.1.call-update) | async-done | bytes 4194320 | tf_op jit(solution)/shard_map/all_gather | solution.py:141
  452.2 9.8 %fusion.44 = bf16[8,64,1,4,128]{4,1,3,0,2:T(8,128)(2,1)S(1)} fusion(f32[8,2048,64,4]{1,2,3,0:T(8,128)} %get-tuple-element.26, f32[8,64,4]{1,2,0:T(4,128)S(1)} %broadcast_maximum_fusion, pred[8,64,2048]{2,1,0:T(8,128)(4,1)S(1)} %compare_and_fusion, bf16[8,2048,128]{2,1,0:T(8,128)(2,1)} %all-gather.12.cloned.1.call-done, f32[8,64,4]{1,2,0:T(4,128)S(1)} %fusion.1), kind=kOutput, calls=%fused_computation.47 | convolution fusion | flops 1095237632 | bytes 22560768 | tf_op jit(solution)/shard_map/gtkjs,gskd->gtkjd/dot_general | solution.py:161
  463.9 6.5 %convolution_convert_fusion = bf16[8,64,4096]{2,1,0:T(8,128)(2,1)} fusion(bf16[8,64,512]{2,1,0:T(8,128)(2,1)S(1)} %reshape.328, bf16[512,4096]{1,0:T(8,128)(2,1)} %param.22), kind=kOutput, calls=%fused_computation.13 | convolution fusion | flops 2149580800 | bytes 8912896 | tf_op jit(solution)/shard_map/gtc,cd->gtd/dot_general | solution.py:184
  470.4 18.1 %all-gather.20.cloned.1.call-done = bf16[8,16,4096]{2,1,0:T(8,128)(2,1)} async-done(((bf16[1,16,4096]{2,1,0:T(8,128)(2,1)}), bf16[8,16,4096]{2,1,0:T(8,128)(2,1)}) %all-gather.20.cloned.1.call-update) | async-done | bytes 1048592 | tf_op jit(solution)/shard_map/all_gather | solution.py:98
  488.6 1.8 gather_fusion.2
  490.4 39.1 %reduce-scatter.5.cloned.1.call-done = bf16[1,64,16]{1,2,0:T(8,128)(2,1)} async-done(((bf16[8,64,16]{1,2,0:T(8,128)(2,1)}), bf16[1,64,16]{1,2,0:T(8,128)(2,1)}) %reduce-scatter.5.cloned.1.call-update) | async-done | bytes 2064 | tf_op jit(solution)/shard_map/reduce_scatter | solution.py:181
  529.5 100.3 %reduce-scatter.3.cloned.1.call-done = bf16[1,64,4096]{2,1,0:T(8,128)(2,1)} async-done(((bf16[8,64,4096]{2,1,0:T(8,128)(2,1)}), bf16[1,64,4096]{2,1,0:T(8,128)(2,1)}) %reduce-scatter.3.cloned.1.call-update) | async-done | bytes 524304 | tf_op jit(solution)/shard_map/reduce_scatter | solution.py:185
  629.8 2.2 fusion.10
  (70 shorter events, 16.9 us)
Async XLA Ops:
  6.5 188.2 %copy-start = (bf16[4096,128]{1,0:T(8,128)(2,1)S(1)}, bf16[4096,128]{1,0:T(8,128)(2,1)}, u32[]{:S(2)}) copy-start(bf16[4096,128]{1,0:T(8,128)(2,1)} %param.20) | copy-start | bytes 3145732
  6.5 86.3 %all-gather.10.cloned.1.call-start = ((), (), s32[]{:S(2)}) async-start(), calls=%async_computation.3 | async-start | bytes 3538944 | tf_op jit(solution)/shard_map/all_gather | solution.py:94
  7.3 181.0 %all-gather.8.cloned.1.call-start = ((), (), s32[]{:S(2)}) async-start(), calls=%async_computation.2 | async-start | bytes 4718592 | tf_op jit(solution)/shard_map/all_gather | solution.py:108
  8.0 220.1 %all-gather.16.cloned.1.call-start = ((), (), s32[]{:S(2)}) async-start(), calls=%async_computation.6 | async-start | bytes 1179648 | tf_op jit(solution)/shard_map/all_gather | solution.py:95
  8.7 263.3 %all-gather.18.cloned.1.call-start = ((), (), s32[]{:S(2)}) async-start(), calls=%async_computation.8 | async-start | bytes 1179648 | tf_op jit(solution)/shard_map/all_gather | solution.py:97
  9.3 356.9 %all-gather.14.cloned.1.call-start = ((), (), s32[]{:S(2)}) async-start(), calls=%async_computation.5 | async-start | bytes 4325376 | tf_op jit(solution)/shard_map/all_gather | solution.py:140
  194.5 6.0 copy-start.2
  200.5 251.8 %all-gather.12.cloned.1.call-start = ((), (), s32[]{:S(2)}) async-start(), calls=%async_computation.4 | async-start | bytes 4325376 | tf_op jit(solution)/shard_map/all_gather | solution.py:141
  204.9 283.7 %all-gather.20.cloned.1.call-start = ((), (), s32[]{:S(2)}) async-start(), calls=%async_computation.10 | async-start | bytes 1179648 | tf_op jit(solution)/shard_map/all_gather | solution.py:98
  205.6 323.9 %reduce-scatter.5.cloned.1.call-start = ((), (), s32[]{:S(2)}) async-start(), calls=%async_computation.9 | async-start | bytes 36864 | tf_op jit(solution)/shard_map/reduce_scatter | solution.py:181
  463.9 165.9 %reduce-scatter.3.cloned.1.call-start = ((), (), s32[]{:S(2)}) async-start(), calls=%async_computation.7 | async-start | bytes 4718592 | tf_op jit(solution)/shard_map/reduce_scatter | solution.py:185
  470.4 161.6 %copy-start.1 = (bf16[4096,128]{1,0:T(8,128)(2,1)S(1)}, bf16[4096,128]{1,0:T(8,128)(2,1)}, u32[]{:S(2)}) copy-start(bf16[4096,128]{1,0:T(8,128)(2,1)} %param.20) | copy-start | bytes 3145732
Sparse Core Ops, SparseCore 0:
  9.1 83.6 all-gather.9
  94.6 93.5 all-gather.7
  190.0 38.0 all-gather.15
  229.8 42.2 all-gather.17
  274.7 91.4 all-gather.13
  368.9 83.2 all-gather.11
  454.0 34.5 all-gather.19
  491.1 38.3 reduce-scatter.4
  532.1 97.6 reduce-scatter.2
where the time goes:
time: 639 us
  waiting for transfers between devices  517 us (81%)
  matrix products  49.3 us (8%)
  blocking collectives  29.5 us (5%)
  other arithmetic  16.3 us (3%)
  between operations  13.5 us (2%)
  local copies, waits for them, and re-layouts  13 us (2%)
    reduce_scatter x1, waiting for transfers between devices, body(): lax.psum_scatter(lax.optimization_barrier(partial_term.astype(jnp.bfloat1...  100 us
    all_gather x1, waiting for transfers between devices, body(): all_requests = lax.all_gather(tokens, 'grp', axis=0, tiled=True)  91.1 us
    all_gather x1, waiting for transfers between devices, body(): key_piece = lax.all_gather(key, 'ctx', axis=1, tiled=True)  84.8 us
    all_gather x1, waiting for transfers between devices, body(): value_piece = lax.all_gather(value, 'ctx', axis=1, tiled=True)  67.4 us
    all_gather x1, waiting for transfers between devices, body(): lax.all_gather(down_qkv, 'grp', axis=0, tiled=True)  49.3 us
    all_gather x1, waiting for transfers between devices, body(): lax.all_gather(down_out, 'grp', axis=0, tiled=True)  42.5 us
    reduce_scatter x1, waiting for transfers between devices, body(): lax.psum_scatter(out_terms.astype(jnp.bfloat16), 'grp', scatter_dimension...  39.1 us
    all_gather x1, blocking collectives, body(): lax.all_gather(up_kv, 'grp', axis=0, tiled=True)  29.5 us
  transfers between devices with their start and end apart: 9, of which 9 were waited for; matrix products, arithmetic and copies ran while one was open for 12% of the time, Pallas kernels for 0%

commit v1 on v0

--- a/solution.py
+++ b/solution.py
@@ -94,7 +94,9 @@
         lax.all_gather(down_qkv, "grp", axis=0, tiled=True),
         lax.all_gather(up_query, "grp", axis=0, tiled=True),
         lax.all_gather(up_kv, "grp", axis=0, tiled=True),
-        lax.all_gather(down_out, "grp", axis=0, tiled=True),
+        jnp.concatenate(
+            lax.all_to_all(jnp.stack([down_out] * lax.axis_size("grp")), "grp", 0, 0), axis=0
+        ),
         lax.all_gather(up_out, "grp", axis=0, tiled=True),
     )
     upq_slots = lax.dynamic_slice_in_dim(upq_slots, group_index * q_cols, q_cols, 2)

time: 639 us -> 601 us (0.941)
  waiting for transfers between devices: 517 us -> 475 us
    all_gather x1 -> x0, waiting for transfers between devices: 42.5 us -> none  [body(): lax.all_gather(down_out, 'grp', axis=0, tiled=True)]
    all_to_all x0 -> x1, waiting for transfers between devices: none -> 24.4 us  [body(): lax.all_to_all(jnp.stack([down_out] * lax.axis_size('grp')), 'grp', 0, 0)]
    all_gather x1, waiting for transfers between devices: 20.7 us -> 0.17 us  [body(): lax.all_gather(up_query, 'grp', axis=0, tiled=True)]
  transfers between devices with their start and end apart: 9 -> 9, of which waited for: 9 -> 9; matrix products, arithmetic and copies ran while one was open for 12% -> 13% of each run, Pallas kernels for 0% -> 0%
where the time goes in v1:
time: 601 us
  waiting for transfers between devices  475 us (79%)
  matrix products  49.3 us (8%)
  blocking collectives  28.9 us (5%)
  other arithmetic  16.3 us (3%)
  between operations  13.8 us (2%)
  local copies, waits for them, and re-layouts  13.2 us (2%)
    reduce_scatter x1, waiting for transfers between devices, body(): lax.psum_scatter(lax.optimization_barrier(partial_term.astype(jnp.bfloat1...  100 us
    all_gather x1, waiting for transfers between devices, body(): all_requests = lax.all_gather(tokens, 'grp', axis=0, tiled=True)  90.5 us
    all_gather x1, waiting for transfers between devices, body(): key_piece = lax.all_gather(key, 'ctx', axis=1, tiled=True)  82.3 us
    all_gather x1, waiting for transfers between devices, body(): value_piece = lax.all_gather(value, 'ctx', axis=1, tiled=True)  67.4 us
    all_gather x1, waiting for transfers between devices, body(): lax.all_gather(down_qkv, 'grp', axis=0, tiled=True)  50.4 us
    reduce_scatter x1, waiting for transfers between devices, body(): lax.psum_scatter(out_terms.astype(jnp.bfloat16), 'grp', scatter_dimension...  39.3 us
    all_gather x1, blocking collectives, body(): lax.all_gather(up_kv, 'grp', axis=0, tiled=True)  28.9 us
    all_to_all x1, waiting for transfers between devices, body(): lax.all_to_all(jnp.stack([down_out] * lax.axis_size('grp')), 'grp', 0, 0)  24.4 us
  transfers between devices with their start and end apart: 9, of which 9 were waited for; matrix products, arithmetic and copies ran while one was open for 13% of the time, Pallas kernels for 0%

profile of v1, /device:TPU:1, one launch (start us, length us, event | category | flops | bytes accessed | tf_op | source)
XLA Modules:
  0.0 600.6 jit_solution(6344678096145553087)
XLA Ops:
  12.7 28.9 %all_gather.23 = bf16[8,2,16,1024]{3,2,1,0:T(8,128)(2,1)S(1)} all-gather(bf16[1,2,16,1024]{3,2,1,0:T(8,128)(2,1)} %param.25), channel_id=1, replica_groups=mesh['grp'=8,'ctx'=32] {'grp'}, dimensions={0}, use_global_device_ids=true | all-gather | bytes 589824 | tf_op jit(solution)/shard_map/all_gather | solution.py:96
  42.4 50.4 %all-gather.9.cloned.1.call-done = bf16[8,48,4096]{2,1,0:T(8,128)(2,1)} async-done(((bf16[1,48,4096]{2,1,0:T(8,128)(2,1)}), bf16[8,48,4096]{2,1,0:T(8,128)(2,1)}) %all-gather.9.cloned.1.call-update) | async-done | bytes 3145744 | tf_op jit(solution)/shard_map/all_gather | solution.py:94
  92.8 4.3 gather_fusion
  97.1 90.5 %all-gather.7.cloned.1.call-done = bf16[8,64,4096]{2,1,0:T(8,128)(2,1)} async-done(((bf16[1,64,4096]{2,1,0:T(8,128)(2,1)}), bf16[8,64,4096]{2,1,0:T(8,128)(2,1)}) %all-gather.7.cloned.1.call-update) | async-done | bytes 4194320 | tf_op jit(solution)/shard_map/all_gather | solution.py:110
  187.6 6.2 %fusion.20 = bf16[8,64,48]{1,2,0:T(8,128)(2,1)S(1)} fusion(bf16[8,64,4096]{2,1,0:T(8,128)(2,1)} %all-gather.7.cloned.1.call-done, bf16[8,48,4096]{2,1,0:T(8,128)(2,1)} %gather_fusion, pred[8]{0:T(512)(128)(4,1)S(1)} %compare_and_fusion.1, f32[8,64,8]{1,0,2:T(8,128)S(1)} %copy.47), kind=kOutput, calls=%fused_computation.30 | convolution fusion | flops 1612554240 | bytes 7405576 | tf_op jit(solution)/shard_map/gtd,afd->gtaf/dot_general | solution.py:55
  194.1 3.5 fusion.88
  197.9 1.2 fusion.58
  200.0 3.5 fusion.87
  204.3 1.1 stack.2
  205.4 3.8 all-to-all-start
  211.5 24.4 %all-to-all-done = bf16[8,1,16,4096]{3,2,1,0:T(8,128)(2,1)S(1)} async-done(((bf16[8,1,16,4096]{3,2,1,0:T(8,128)(2,1)}), bf16[8,1,16,4096]{3,2,1,0:T(8,128)(2,1)S(1)}, u32[]{:S(2)}, u32[]{:S(2)}) %all-to-all-start) | async-done | bytes 1048608 | tf_op jit(solution)/shard_map/all_to_all | solution.py:98
  236.7 0.9 constant_dynamic-slice_fusion
  238.2 5.8 fusion.89
  246.1 82.3 %all-gather.13.cloned.1.call-done = bf16[8,2048,128]{2,1,0:T(8,128)(2,1)} async-done(((bf16[8,64,128]{2,1,0:T(8,128)(2,1)}), bf16[8,2048,128]{2,1,0:T(8,128)(2,1)}) %all-gather.13.cloned.1.call-update) | async-done | bytes 4194320 | tf_op jit(solution)/shard_map/all_gather | solution.py:142
  328.3 10.0 %fusion = (f32[8,64,4]{1,2,0:T(4,128)S(1)}, f32[8,2048,64,4]{1,2,3,0:T(8,128)}) fusion(pred[8,64,2048]{2,1,0:T(8,128)(4,1)S(1)} %compare_and_fusion, bf16[8,64,4,64]{3,1,2,0:T(8,128)(2,1)S(1)} %copy.52, bf16[8,64,4,64]{3,1,2,0:T(8,128)(2,1)S(1)} %copy.51, bf16[8,2048,128]{2,1,0:T(8,128)(2,1)} %all-gather.13.cloned.1.call-done), kind=kOutput, calls=%fused_computation.7 | convolution fusion | flops 1087371264 | bytes 22552576 | tf_op jit(solution)/shard_map/gtkjd,gskd->gtkjs/dot_general | solution.py:155
  338.3 8.7 %fusion.1 = f32[8,64,4]{1,2,0:T(4,128)S(1)} fusion(f32[8,2048,64,4]{1,2,3,0:T(8,128)} %get-tuple-element.26, f32[8,64,4]{1,2,0:T(4,128)S(1)} %broadcast_maximum_fusion, pred[8,64,2048]{2,1,0:T(8,128)(4,1)S(1)} %compare_and_fusion), kind=kLoop, calls=%fused_computation.8 | loop fusion | flops 20969472 | bytes 17842176 | tf_op jit(solution)/shard_map/reduce_sum | solution.py:162
  347.0 67.4 %all-gather.11.cloned.1.call-done = bf16[8,2048,128]{2,1,0:T(8,128)(2,1)} async-done(((bf16[8,64,128]{2,1,0:T(8,128)(2,1)}), bf16[8,2048,128]{2,1,0:T(8,128)(2,1)}) %all-gather.11.cloned.1.call-update) | async-done | bytes 4194320 | tf_op jit(solution)/shard_map/all_gather | solution.py:143
  414.3 9.8 %fusion.44 = bf16[8,64,1,4,128]{4,1,3,0,2:T(8,128)(2,1)S(1)} fusion(f32[8,2048,64,4]{1,2,3,0:T(8,128)} %get-tuple-element.26, f32[8,64,4]{1,2,0:T(4,128)S(1)} %broadcast_maximum_fusion, pred[8,64,2048]{2,1,0:T(8,128)(4,1)S(1)} %compare_and_fusion, bf16[8,2048,128]{2,1,0:T(8,128)(2,1)} %all-gather.11.cloned.1.call-done, f32[8,64,4]{1,2,0:T(4,128)S(1)} %fusion.1), kind=kOutput, calls=%fused_computation.47 | convolution fusion | flops 1095237632 | bytes 22560768 | tf_op jit(solution)/shard_map/gtkjs,gskd->gtkjd/dot_general | solution.py:163
  426.0 6.5 %convolution_convert_fusion = bf16[8,64,4096]{2,1,0:T(8,128)(2,1)} fusion(bf16[8,64,512]{2,1,0:T(8,128)(2,1)S(1)} %reshape.333, bf16[512,4096]{1,0:T(8,128)(2,1)} %param.22), kind=kOutput, calls=%fused_computation.13 | convolution fusion | flops 2149580800 | bytes 8912896 | tf_op jit(solution)/shard_map/gtc,cd->gtd/dot_general | solution.py:186
  432.6 17.6 %all-gather.17.cloned.1.call-done = bf16[8,16,4096]{2,1,0:T(8,128)(2,1)} async-done(((bf16[1,16,4096]{2,1,0:T(8,128)(2,1)}), bf16[8,16,4096]{2,1,0:T(8,128)(2,1)}) %all-gather.17.cloned.1.call-update) | async-done | bytes 1048592 | tf_op jit(solution)/shard_map/all_gather | solution.py:100
  450.2 1.8 gather_fusion.2
  452.0 39.3 %reduce-scatter.5.cloned.1.call-done = bf16[1,64,16]{1,2,0:T(8,128)(2,1)} async-done(((bf16[8,64,16]{1,2,0:T(8,128)(2,1)}), bf16[1,64,16]{1,2,0:T(8,128)(2,1)}) %reduce-scatter.5.cloned.1.call-update) | async-done | bytes 2064 | tf_op jit(solution)/shard_map/reduce_scatter | solution.py:183
  491.3 100.2 %reduce-scatter.3.cloned.1.call-done = bf16[1,64,4096]{2,1,0:T(8,128)(2,1)} async-done(((bf16[8,64,4096]{2,1,0:T(8,128)(2,1)}), bf16[1,64,4096]{2,1,0:T(8,128)(2,1)}) %reduce-scatter.3.cloned.1.call-update) | async-done | bytes 524304 | tf_op jit(solution)/shard_map/reduce_scatter | solution.py:187
  591.5 2.2 fusion.10
  (72 shorter events, 16.4 us)
Async XLA Ops:
  6.5 187.6 %copy-start = (bf16[4096,128]{1,0:T(8,128)(2,1)S(1)}, bf16[4096,128]{1,0:T(8,128)(2,1)}, u32[]{:S(2)}) copy-start(bf16[4096,128]{1,0:T(8,128)(2,1)} %param.20) | copy-start | bytes 3145732
  6.5 86.3 %all-gather.9.cloned.1.call-start = ((), (), s32[]{:S(2)}) async-start(), calls=%async_computation.4 | async-start | bytes 3538944 | tf_op jit(solution)/shard_map/all_gather | solution.py:94
  7.3 180.4 %all-gather.7.cloned.1.call-start = ((), (), s32[]{:S(2)}) async-start(), calls=%async_computation.3 | async-start | bytes 4718592 | tf_op jit(solution)/shard_map/all_gather | solution.py:110
  8.0 228.7 %all-gather.15.cloned.1.call-start = ((), (), s32[]{:S(2)}) async-start(), calls=%async_computation.7 | async-start | bytes 1179648 | tf_op jit(solution)/shard_map/all_gather | solution.py:95
  8.7 319.6 %all-gather.13.cloned.1.call-start = ((), (), s32[]{:S(2)}) async-start(), calls=%async_computation.6 | async-start | bytes 4325376 | tf_op jit(solution)/shard_map/all_gather | solution.py:142
  193.9 6.1 %copy-start.2 = (bf16[4096,128]{1,0:T(8,128)(2,1)S(1)}, bf16[4096,128]{1,0:T(8,128)(2,1)}, u32[]{:S(2)}) copy-start(bf16[4096,128]{1,0:T(8,128)(2,1)} %param.21) | copy-start | bytes 3145732
  197.6 6.7 %copy-start.3 = (bf16[1,16,4096]{2,1,0:T(8,128)(2,1)S(1)}, bf16[1,16,4096]{2,1,0:T(8,128)(2,1)}, u32[]{:S(2)}) copy-start(bf16[1,16,4096]{2,1,0:T(8,128)(2,1)} %param.26) | copy-start | bytes 393220
  199.9 214.4 %all-gather.11.cloned.1.call-start = ((), (), s32[]{:S(2)}) async-start(), calls=%async_computation.5 | async-start | bytes 4325376 | tf_op jit(solution)/shard_map/all_gather | solution.py:143
  205.4 30.5 %all-to-all-start = ((bf16[8,1,16,4096]{3,2,1,0:T(8,128)(2,1)}), bf16[8,1,16,4096]{3,2,1,0:T(8,128)(2,1)S(1)}, u32[]{:S(2)}, u32[]{:S(2)}) async-start(bf16[8,1,16,4096]{3,2,1,0:T(8,128)(2,1)} %stack.2), calls=%async_computation.1 | async-start | bytes 2097152 | tf_op jit(solution)/shard_map/all_to_all | solution.py:98
  209.2 240.9 %all-gather.17.cloned.1.call-start = ((), (), s32[]{:S(2)}) async-start(), calls=%async_computation.10 | async-start | bytes 1179648 | tf_op jit(solution)/shard_map/all_gather | solution.py:100
  209.8 281.6 %reduce-scatter.5.cloned.1.call-start = ((), (), s32[]{:S(2)}) async-start(), calls=%async_computation.9 | async-start | bytes 36864 | tf_op jit(solution)/shard_map/reduce_scatter | solution.py:183
  426.0 165.5 %reduce-scatter.3.cloned.1.call-start = ((), (), s32[]{:S(2)}) async-start(), calls=%async_computation.8 | async-start | bytes 4718592 | tf_op jit(solution)/shard_map/reduce_scatter | solution.py:187
  432.5 161.2 %copy-start.1 = (bf16[4096,128]{1,0:T(8,128)(2,1)S(1)}, bf16[4096,128]{1,0:T(8,128)(2,1)}, u32[]{:S(2)}) copy-start(bf16[4096,128]{1,0:T(8,128)(2,1)} %param.20) | copy-start | bytes 3145732
Sparse Core Ops, SparseCore 0:
  9.1 83.6 all-gather.8
  94.6 93.0 all-gather.6
  189.4 47.2 all-gather.14
  239.4 88.8 all-gather.12
  331.0 83.2 all-gather.10
  416.0 34.1 all-gather.16
  452.6 38.6 reduce-scatter.4
  493.9 97.6 reduce-scatter.2
